TPU v7x, 128 devices: a whole 4x4x4 slice. The times are simulated.
128 devices in a mesh: src: 8 (over y_lo, x), tgt: 16 (over z, y_hi, core).
Axes of the slice: x: 4, y: 4 (y_hi: 2, y_lo: 2; y = y_hi * 2 + y_lo), z: 4, core: 2. Of those that a mesh axis runs over, the one named last changes fastest.
Arguments:
- residual: bfloat16 [4, 512, 2304], replicated, may hold values from -6 to 6
- targets: bfloat16 [4, 2304, 512], P(None, 'tgt'), may hold values from -6 to 6
- enc_weight: bfloat16 [4, 2304, 16384], P(None, None, ('src', 'tgt')), may hold values from -0.125 to 0.125
- enc_bias: float32 [4, 16384], P(None, ('src', 'tgt')), may hold values from -3 to 3
- active: int32 [4, 512, 16384], P(None, None, ('src', 'tgt')), may hold values 0 or 1
- dec_weight: bfloat16 [80, 2304, 2048], P('src', 'tgt'), may hold values from -0.046875 to 0.046875
- dec_bias: float32 [4, 2304], P(None, 'tgt'), may hold values from -3 to 3
- tile_pairs: int32 [80, 2], P('src'), may hold values from 0 to 3, as said below
Outputs:
- dec_grad: bfloat16 [80, 2304, 2048], P('src', 'tgt')
- enc_grad: bfloat16 [4, 2304, 16384], P(None, None, ('src', 'tgt'))
- bias_grad: float32 [4, 16384], P(None, ('src', 'tgt'))
Inputs may be any that keep to these rules, and one draw needn't show every extreme that they name: `tile_pairs`: rows b * 10 to (b + 1) * 10 - 1 serve latent block b; among them each pair (source, target) with source <= target appears exactly once, source in column 0 and target in column 1.
All inputs are finite; a program needn't handle non-finite values. No bound on the sum of `active` on one device may be relied on, other than what follows from the above.
Results may differ from a plain program's by a relative error of at most 0.019.
Values may be sent and summed in bfloat16 or wider, within the bound.
A program may use at most 128 MiB of HBM per device.

v0:
```python
import jax
import jax.numpy as jnp
from jax import lax
from jax.sharding import PartitionSpec as P


def select_layer(array, index):
    return lax.dynamic_index_in_dim(array, index, 0, keepdims=False)


def add_layer(total, index, value):
    current = lax.dynamic_slice_in_dim(total, index, 1, 0)
    return lax.dynamic_update_slice_in_dim(total, current + value[None], index, 0)


def decoder_term(error_rows, lat_block):
    product = lax.dot_general(
        error_rows, lat_block, (((1,), (0,)), ((), ())), preferred_element_type=jnp.float32
    )
    return product.astype(jnp.bfloat16)


def shards(residual, targets, enc_weight, enc_bias, active, dec_weight, dec_bias, tile_pairs):
    layers = residual.shape[0]
    tok_all = residual.shape[1]
    width_part = targets.shape[1]
    block_width = dec_weight.shape[2]
    mask_own = active.astype(jnp.float32)
    preact = jnp.einsum("lrd,ldc->lrc", residual, enc_weight, preferred_element_type=jnp.float32)
    latent = ((preact + enc_bias[:, None, :]) * mask_own).astype(jnp.bfloat16)
    blocks = lax.all_gather(latent, "tgt", axis=2, tiled=True)
    source_ids = tile_pairs[:, 0]
    target_ids = tile_pairs[:, 1]

    def add_recon(recon_sum, slot_data):
        weight, source, target = slot_data
        lat_block = select_layer(blocks, source)
        recon_term = lax.dot_general(
            weight, lat_block, (((1,), (1,)), ((), ())), preferred_element_type=jnp.float32
        )
        return (add_layer(recon_sum, target, recon_term), None)

    recon_zero = jnp.zeros((layers, width_part, tok_all), jnp.float32)
    recon_sum = lax.scan(add_recon, recon_zero, (dec_weight, source_ids, target_ids))[0]
    whole_sum = lax.psum(recon_sum.astype(jnp.bfloat16), "src").astype(jnp.float32)
    error_part = (whole_sum + dec_bias[:, :, None] - targets.astype(jnp.float32)).astype(
        jnp.bfloat16
    )

    def step_partial(grad_sum, slot_data):
        weight, source, target = slot_data
        error_rows = select_layer(error_part, target)
        lat_block = select_layer(blocks, source)
        lat_term = lax.dot_general(
            error_rows, weight, (((0,), (0,)), ((), ())), preferred_element_type=jnp.float32
        )
        return (add_layer(grad_sum, source, lat_term), decoder_term(error_rows, lat_block))

    grad_zero = jnp.zeros((layers, tok_all, block_width), jnp.float32)
    grad_sum, dec_grad = lax.scan(step_partial, grad_zero, (dec_weight, source_ids, target_ids))
    owned_grad = lax.psum_scatter(
        grad_sum.astype(jnp.bfloat16), "tgt", scatter_dimension=2, tiled=True
    ).astype(jnp.float32)
    pre_grad = (owned_grad * mask_own).astype(jnp.bfloat16)
    enc_grad = jnp.einsum(
        "lrd,lrc->ldc", residual, pre_grad, preferred_element_type=jnp.float32
    ).astype(jnp.bfloat16)
    bias_grad = jnp.sum(pre_grad.astype(jnp.float32), axis=1)
    return (dec_grad, enc_grad, bias_grad)


def solution(mesh):
    in_specs = (
        P(),
        P(None, "tgt", None),
        P(None, None, ("src", "tgt")),
        P(None, ("src", "tgt")),
        P(None, None, ("src", "tgt")),
        P("src", "tgt", None),
        P(None, "tgt"),
        P("src", None),
    )
    out_specs = (P("src", "tgt", None), P(None, None, ("src", "tgt")), P(None, ("src", "tgt")))
    return jax.shard_map(shards, mesh=mesh, in_specs=in_specs, out_specs=out_specs, check_vma=False)
```

profile of v0, /device:TPU:0, one launch (start us, length us, event | category | flops | bytes accessed | tf_op | source)
XLA Modules:
  0.0 544.1 jit_solution(14176928572429023302)
XLA Ops:
  8.8 7.4 %fusion.30 = bf16[4,512,128]{2,1,0:T(8,128)(2,1)} fusion(bf16[4,512,2304]{2,1,0:T(8,128)(2,1)} %param.12, bf16[4,2304,128]{2,1,0:T(8,128)(2,1)S(1)} %copy-done, s32[4,512,128]{2,1,0:T(8,128)} %param.16, f32[4,128]{1,0:T(4,128)} %param.15), kind=kOutput, calls=%fused_computation.28 | convolution fusion | flops 1209008128 | bytes 13371392 | tf_op jit(solution)/shard_map/lrd,ldc->lrc/dot_general | solution.py:29
  16.4 79.1 %all-gather.2.cloned.1.call-done = bf16[4,512,2048]{2,1,0:T(8,128)(2,1)} async-done(((bf16[4,512,128]{2,1,0:T(8,128)(2,1)}), bf16[4,512,2048]{2,1,0:T(8,128)(2,1)}) %all-gather.2.cloned.1.call-update) | async-done | bytes 8388624 | tf_op jit(solution)/shard_map/all_gather | solution.py:31
  95.7 77.2 %while.22 = (s32[]{:T(128)}, f32[4,144,512]{2,1,0:T(8,128)S(1)}, s32[10]{0:T(128)S(1)}, bf16[10,144,2048]{2,1,0:T(8,128)(2,1)}, s32[10]{0:T(128)S(1)}, /*index=5...) while((s32[]{:T(128)}, f32[4,144,512]{2,1,0:T(8,128)S(1)}, s32[10]{0:T(128)S(1)}, ...), condition=%wide.region_1.2_spmd, body=%wide.region_0.1_spmd.sunk | while | flops 302063616 | bytes 3277005 | solution.py:44
  174.0 72.7 %all-reduce.2.cloned.1.call-done = bf16[4,144,512]{2,1,0:T(8,128)(2,1)} async-done(((bf16[4,144,512]{2,1,0:T(8,128)(2,1)}), bf16[4,144,512]{2,1,0:T(8,128)(2,1)}) %all-reduce.2.cloned.1.call-update) | async-done | bytes 589840 | tf_op jit(solution)/shard_map/psum | solution.py:45
  248.1 7.9 %broadcast_in_dim.21 = f32[4,512,2048]{2,1,0:T(8,128)} broadcast(f32[]{:T(128)} %constant.31.clone.1), dimensions={} | broadcast | bytes 16777220 | tf_op jit(solution)/shard_map/broadcast_in_dim | solution.py:59
  255.9 130.4 %while.23 = (s32[]{:T(128)}, f32[4,512,2048]{2,1,0:T(8,128)}, bf16[10,144,2048]{2,1,0:T(8,128)(2,1)}, s32[10]{0:T(128)S(1)}, s32[10]{0:T(128)S(1)}, /*index=5*/b...) while((s32[]{:T(128)}, f32[4,512,2048]{2,1,0:T(8,128)}, ...), condition=%wide.region_4.5_spmd, body=%wide.region_3.4_spmd.sunk | while | flops 605323264 | bytes 11960553 | solution.py:60
  263.9 5.1 fusion.50
  276.9 5.1 fusion.50
  289.9 5.1 fusion.50
  303.0 5.1 fusion.50
  316.0 5.1 fusion.50
  326.2 2.9 fusion.51
  329.1 5.1 fusion.50
  342.1 5.1 fusion.50
  352.2 2.9 fusion.51
  355.1 5.1 fusion.50
  368.2 5.1 fusion.50
  381.3 5.1 fusion.50
  386.3 9.1 %convert_element_type.45 = bf16[4,512,2048]{2,1,0:T(8,128)(2,1)} convert(f32[4,512,2048]{2,1,0:T(8,128)} %get-tuple-element.80) | non-fusion elementwise | flops 4194304 | bytes 25165824 | tf_op jit(solution)/shard_map/convert_element_type | solution.py:62
  395.4 14.6 %copy.16 = bf16[4,512,2048]{1,0,2:T(4,128)(2,1)} copy(bf16[4,512,2048]{2,1,0:T(8,128)(2,1)} %convert_element_type.45) | data formatting | bytes 16777216
  410.0 10.2 %copy.18 = bf16[256,8,4,512]{3,1,2,0:T(8,128)(2,1)} copy(bf16[256,8,4,512]{3,2,1,0:T(4,128)(2,1)} %bitcast.81) | data formatting | bytes 16777216
  420.3 102.1 %reduce-scatter.4.cloned.1.call-done = bf16[128,2048]{1,0:T(8,128)(2,1)} async-done(((bf16[2048,2048]{1,0:T(8,128)(2,1)}), bf16[128,2048]{1,0:T(8,128)(2,1)}) %reduce-scatter.4.cloned.1.call-update) | async-done | bytes 524304
  526.4 6.9 %fusion.28 = bf16[4,2304,128]{1,2,0:T(8,128)(2,1)} fusion(bf16[4,512,2304]{2,1,0:T(8,128)(2,1)} %param.12, bf16[4,512,128]{2,1,0:T(8,128)(2,1)S(1)} %copy.17, s32[4,512,128]{2,1,0:T(8,128)} %param.16), kind=kOutput, calls=%fused_computation.25 | convolution fusion | flops 1210187776 | bytes 13369344 | tf_op jit(solution)/shard_map/lrd,lrc->ldc/dot_general | solution.py:65
  533.3 4.3 copy.14
  (82 shorter events, 81.3 us)
Async XLA Ops:
  7.2 1.7 copy-start
  7.2 9.2 %copy-start.4 = (s32[10,2]{0,1:T(2,128)S(1)}, s32[10,2]{0,1:T(2,128)}, u32[]{:S(2)}) copy-start(s32[10,2]{0,1:T(2,128)} %param.19) | copy-start | bytes 244
  7.2 88.3 %all-gather.2.cloned.1.call-start = ((), (), s32[]{:S(2)}) async-start(), calls=%async_computation.1 | async-start | bytes 8912896 | tf_op jit(solution)/shard_map/all_gather | solution.py:31
  16.3 230.4 %all-reduce.2.cloned.1.call-start = ((), (), s32[]{:S(2)}) async-start(), calls=%async_computation.2 | async-start | bytes 1179648 | tf_op jit(solution)/shard_map/psum | solution.py:45
  95.7 151.1 %copy-start.2 = (bf16[4,144,512]{2,1,0:T(8,128)(2,1)S(1)}, bf16[4,144,512]{2,1,0:T(8,128)(2,1)}, u32[]{:S(2)}) copy-start(bf16[4,144,512]{2,1,0:T(8,128)(2,1)} %param.13) | copy-start | bytes 1769476
  95.7 151.1 %copy-start.3 = (f32[4,144]{1,0:T(4,128)S(1)}, f32[4,144]{1,0:T(4,128)}, u32[]{:S(2)}) copy-start(f32[4,144]{1,0:T(4,128)} %param.18) | copy-start | bytes 6916
  173.8 348.6 %reduce-scatter.4.cloned.1.call-start = ((), (), s32[]{:S(2)}) async-start(), calls=%async_computation.3 | async-start | bytes 8912896
  524.3 13.3 %copy-start.1 = (bf16[4,2304,128]{2,1,0:T(8,128)(2,1)S(1)}, bf16[4,2304,128]{2,1,0:T(8,128)(2,1)}, u32[]{:S(2)}) copy-start(bf16[4,2304,128]{2,1,0:T(8,128)(2,1)} %param.14) | copy-start | bytes 7077892
Sparse Core Ops, SparseCore 0:
  16.4 79.0 all-gather.1
  173.9 72.7 all-reduce.1
  420.4 101.9 reduce-scatter.3
where the time goes:
time: 547 us; the launch traced here: 544 us
  waiting for transfers between devices  254 us (46%)
  matrix products  121 us (22%)
  loops' own time  78 us (14%)
  local copies, waits for them, and re-layouts  64 us (12%)
  between operations  13.8 us (3%)
  other arithmetic  13.4 us (2%)
    unnamed x4, waiting for transfers between devices  102 us
    all_gather x1, waiting for transfers between devices, shards(): blocks = lax.all_gather(latent, 'tgt', axis=2, tiled=True)  79.1 us
    psum x1, waiting for transfers between devices, shards(): lax.psum(recon_sum.astype(jnp.bfloat16), 'src').astype(jnp.float32)  72.7 us
    dot_general x10, matrix products, step_partial(): lax.dot_general(error_rows, weight, (((0,), (0,)), ((), ())), preferred_e...  50.8 us
    another operation x1, loops' own time, shards(): lax.scan(add_recon, recon_zero, (dec_weight, source_ids, target_ids))[0]  39.1 us
    another operation x1, loops' own time, shards(): lax.scan(step_partial, grad_zero, (dec_weight, source_ids, target_ids))  38.9 us
    unnamed x15, local copies, waits for them, and re-layouts  32.6 us
    dot_general x10, matrix products, decoder_term(): lax.dot_general(error_rows, lat_block, (((1,), (0,)), ((), ())), preferre...  29 us
  transfers between devices with their start and end apart: 3, of which 3 were waited for; matrix products, arithmetic and copies ran while one was open for 0% of the time, Pallas kernels for 0%

commit v1 on v0

--- a/solution.py
+++ b/solution.py
@@ -28,7 +28,9 @@
     mask_own = active.astype(jnp.float32)
     preact = jnp.einsum("lrd,ldc->lrc", residual, enc_weight, preferred_element_type=jnp.float32)
     latent = ((preact + enc_bias[:, None, :]) * mask_own).astype(jnp.bfloat16)
-    blocks = lax.all_gather(latent, "tgt", axis=2, tiled=True)
+    blocks = jnp.concatenate(
+        lax.all_to_all(jnp.stack([latent] * lax.axis_size("tgt")), "tgt", 0, 0), axis=2
+    )
     source_ids = tile_pairs[:, 0]
     target_ids = tile_pairs[:, 1]
 

time: 547 us -> 601 us (1.099)
  local copies, waits for them, and re-layouts: 64 us -> 92.2 us
  waiting for transfers between devices: 254 us -> 272 us
  starting transfers between devices: 0.3 us -> 8.61 us
    all_to_all x0 -> x1, waiting for transfers between devices: none -> 96.7 us  [shards(): lax.all_to_all(jnp.stack([latent] * lax.axis_size('tgt')), 'tgt', 0, 0)]
    all_gather x1 -> x0, waiting for transfers between devices: 79.1 us -> none  [shards(): blocks = lax.all_gather(latent, 'tgt', axis=2, tiled=True)]
    while x0 -> x1, local copies, waits for them, and re-layouts: none -> 11.5 us  [shards(): lax.scan(add_recon, recon_zero, (dec_weight, source_ids, target_ids))[0]]
    all_to_all x0 -> x1, local copies, waits for them, and re-layouts: none -> 11.4 us  [shards(): lax.all_to_all(jnp.stack([latent] * lax.axis_size('tgt')), 'tgt', 0, 0)]
    all_to_all x0 -> x1, starting transfers between devices: none -> 8.34 us  [shards(): lax.all_to_all(jnp.stack([latent] * lax.axis_size('tgt')), 'tgt', 0, 0)]
    unnamed x4 -> x3, waiting for transfers between devices: 102 us -> 102 us
where the time goes in v1:
time: 601 us; the launch traced here: 598 us
  waiting for transfers between devices  272 us (45%)
  matrix products  120 us (20%)
  local copies, waits for them, and re-layouts  92.2 us (15%)
  loops' own time  78 us (13%)
  between operations  14.1 us (2%)
  other arithmetic  13.4 us (2%)
  starting transfers between devices  8.61 us (1%)
    unnamed x3, waiting for transfers between devices  102 us
    all_to_all x1, waiting for transfers between devices, shards(): lax.all_to_all(jnp.stack([latent] * lax.axis_size('tgt')), 'tgt', 0, 0)  96.7 us
    psum x1, waiting for transfers between devices, shards(): lax.psum(recon_sum.astype(jnp.bfloat16), 'src').astype(jnp.float32)  72.8 us
    dot_general x10, matrix products, step_partial(): lax.dot_general(error_rows, weight, (((0,), (0,)), ((), ())), preferred_e...  50.9 us
    another operation x1, loops' own time, shards(): lax.scan(add_recon, recon_zero, (dec_weight, source_ids, target_ids))[0]  39.1 us
    another operation x1, loops' own time, shards(): lax.scan(step_partial, grad_zero, (dec_weight, source_ids, target_ids))  38.9 us
    unnamed x15, local copies, waits for them, and re-layouts  32.6 us
    dot_general x10, matrix products, decoder_term(): lax.dot_general(error_rows, lat_block, (((1,), (0,)), ((), ())), preferre...  29 us
  transfers between devices with their start and end apart: 3, of which 3 were waited for; matrix products, arithmetic and copies ran while one was open for 0% of the time, Pallas kernels for 0%

profile of v1, /device:TPU:0, one launch (start us, length us, event | category | flops | bytes accessed | tf_op | source)
XLA Modules:
  0.0 597.6 jit_solution(13098670512011797560)
XLA Ops:
  8.8 6.6 %fusion.30 = bf16[4,512,128]{2,1,0:T(8,128)(2,1)S(1)} fusion(bf16[4,512,2304]{2,1,0:T(8,128)(2,1)} %param.12, bf16[4,2304,128]{2,1,0:T(8,128)(2,1)S(1)} %copy-done, s32[4,512,128]{2,1,0:T(8,128)} %param.16, f32[4,128]{1,0:T(4,128)} %param.15), kind=kOutput, calls=%fused_computation.28 | convolution fusion | flops 1209008128 | bytes 13371392 | tf_op jit(solution)/shard_map/lrd,ldc->lrc/dot_general | solution.py:29
  15.5 5.2 stack.2
  20.7 8.3 %all-to-all-start = ((bf16[16,4,512,128]{3,2,1,0:T(8,128)(2,1)}), bf16[16,4,512,128]{3,2,1,0:T(8,128)(2,1)}, u32[]{:S(2)}, u32[]{:S(2)}) async-start(bf16[16,4,512,128]{3,2,1,0:T(8,128)(2,1)} %stack.2), calls=%async_computation | async-start | bytes 16777216 | tf_op jit(solution)/shard_map/all_to_all | solution.py:32
  29.2 96.7 %all-to-all-done = bf16[16,4,512,128]{3,2,1,0:T(8,128)(2,1)} async-done(((bf16[16,4,512,128]{3,2,1,0:T(8,128)(2,1)}), bf16[16,4,512,128]{3,2,1,0:T(8,128)(2,1)}, u32[]{:S(2)}, u32[]{:S(2)}) %all-to-all-start) | async-done | bytes 8388640 | tf_op jit(solution)/shard_map/all_to_all | solution.py:32
  125.8 11.4 %copy.15 = bf16[16,4,512,128]{2,3,0,1:T(8,128)(2,1)} copy(bf16[16,4,512,128]{3,2,1,0:T(8,128)(2,1)} %all-to-all-done) | data formatting | bytes 16777216 | tf_op jit(solution)/shard_map/all_to_all | solution.py:32
  137.3 11.5 %copy.16 = bf16[4,512,2048]{2,1,0:T(8,128)(2,1)} copy(bf16[4,512,2048]{1,2,0:T(8,128)(2,1)} %bitcast.84) | data formatting | bytes 16777216 | tf_op jit(solution)/shard_map/while | solution.py:46
  148.9 77.2 %while.22 = (s32[]{:T(128)}, f32[4,144,512]{2,1,0:T(8,128)S(1)}, s32[10]{0:T(128)S(1)}, bf16[10,144,2048]{2,1,0:T(8,128)(2,1)}, s32[10]{0:T(128)S(1)}, /*index=5...) while((s32[]{:T(128)}, f32[4,144,512]{2,1,0:T(8,128)S(1)}, s32[10]{0:T(128)S(1)}, ...), condition=%wide.region_1.2_spmd, body=%wide.region_0.1_spmd.sunk | while | flops 302063616 | bytes 3277005 | solution.py:46
  227.2 72.8 %all-reduce.2.cloned.1.call-done = bf16[4,144,512]{2,1,0:T(8,128)(2,1)} async-done(((bf16[4,144,512]{2,1,0:T(8,128)(2,1)}), bf16[4,144,512]{2,1,0:T(8,128)(2,1)}) %all-reduce.2.cloned.1.call-update) | async-done | bytes 589840 | tf_op jit(solution)/shard_map/psum | solution.py:47
  301.4 7.9 %broadcast_in_dim.21 = f32[4,512,2048]{2,1,0:T(8,128)} broadcast(f32[]{:T(128)} %constant.31.clone.1), dimensions={} | broadcast | bytes 16777220 | tf_op jit(solution)/shard_map/broadcast_in_dim | solution.py:61
  309.2 130.5 %while.23 = (s32[]{:T(128)}, f32[4,512,2048]{2,1,0:T(8,128)}, bf16[10,144,2048]{2,1,0:T(8,128)(2,1)}, s32[10]{0:T(128)S(1)}, s32[10]{0:T(128)S(1)}, /*index=5*/b...) while((s32[]{:T(128)}, f32[4,512,2048]{2,1,0:T(8,128)}, ...), condition=%wide.region_4.5_spmd, body=%wide.region_3.4_spmd.sunk | while | flops 605323264 | bytes 11960553 | solution.py:62
  317.2 5.1 fusion.50
  330.2 5.1 fusion.50
  343.2 5.1 fusion.50
  369.3 5.1 fusion.50
  382.4 5.1 fusion.50
  395.4 5.1 fusion.50
  408.5 5.1 fusion.50
  421.5 5.1 fusion.50
  434.6 5.1 fusion.50
  439.7 9.1 %convert_element_type.45 = bf16[4,512,2048]{2,1,0:T(8,128)(2,1)} convert(f32[4,512,2048]{2,1,0:T(8,128)} %get-tuple-element.80) | non-fusion elementwise | flops 4194304 | bytes 25165824 | tf_op jit(solution)/shard_map/convert_element_type | solution.py:64
  448.8 14.5 %copy.21 = bf16[4,512,2048]{1,0,2:T(4,128)(2,1)} copy(bf16[4,512,2048]{2,1,0:T(8,128)(2,1)} %convert_element_type.45) | data formatting | bytes 16777216
  463.3 10.2 %copy.23 = bf16[256,8,4,512]{3,1,2,0:T(8,128)(2,1)} copy(bf16[256,8,4,512]{3,2,1,0:T(4,128)(2,1)} %bitcast.85) | data formatting | bytes 16777216
  473.6 102.1 %reduce-scatter.4.cloned.1.call-done = bf16[128,2048]{1,0:T(8,128)(2,1)} async-done(((bf16[2048,2048]{1,0:T(8,128)(2,1)}), bf16[128,2048]{1,0:T(8,128)(2,1)}) %reduce-scatter.4.cloned.1.call-update) | async-done | bytes 524304
  579.6 6.9 %fusion.28 = bf16[4,2304,128]{1,2,0:T(8,128)(2,1)} fusion(bf16[4,512,2304]{2,1,0:T(8,128)(2,1)} %param.12, bf16[4,512,128]{2,1,0:T(8,128)(2,1)S(1)} %copy.22, s32[4,512,128]{2,1,0:T(8,128)} %param.16), kind=kOutput, calls=%fused_computation.25 | convolution fusion | flops 1210187776 | bytes 13369344 | tf_op jit(solution)/shard_map/lrd,lrc->ldc/dot_general | solution.py:67
  (84 shorter events, 96.4 us)
Async XLA Ops:
  7.2 1.7 copy-start
  20.7 8.4 %copy-start.4 = (s32[10,2]{0,1:T(2,128)S(1)}, s32[10,2]{0,1:T(2,128)}, u32[]{:S(2)}) copy-start(s32[10,2]{0,1:T(2,128)} %param.19) | copy-start | bytes 244
  20.7 105.1 %all-to-all-start = ((bf16[16,4,512,128]{3,2,1,0:T(8,128)(2,1)}), bf16[16,4,512,128]{3,2,1,0:T(8,128)(2,1)}, u32[]{:S(2)}, u32[]{:S(2)}) async-start(bf16[16,4,512,128]{3,2,1,0:T(8,128)(2,1)} %stack.2), calls=%async_computation | async-start | bytes 16777216 | tf_op jit(solution)/shard_map/all_to_all | solution.py:32
  29.1 271.0 %all-reduce.2.cloned.1.call-start = ((), (), s32[]{:S(2)}) async-start(), calls=%async_computation.2 | async-start | bytes 1179648 | tf_op jit(solution)/shard_map/psum | solution.py:47
  148.9 151.2 %copy-start.2 = (bf16[4,144,512]{2,1,0:T(8,128)(2,1)S(1)}, bf16[4,144,512]{2,1,0:T(8,128)(2,1)}, u32[]{:S(2)}) copy-start(bf16[4,144,512]{2,1,0:T(8,128)(2,1)} %param.13) | copy-start | bytes 1769476
  148.9 151.2 %copy-start.3 = (f32[4,144]{1,0:T(4,128)S(1)}, f32[4,144]{1,0:T(4,128)}, u32[]{:S(2)}) copy-start(f32[4,144]{1,0:T(4,128)} %param.18) | copy-start | bytes 6916
  227.0 348.7 %reduce-scatter.4.cloned.1.call-start = ((), (), s32[]{:S(2)}) async-start(), calls=%async_computation.3 | async-start | bytes 8912896
  577.5 13.3 %copy-start.1 = (bf16[4,2304,128]{2,1,0:T(8,128)(2,1)S(1)}, bf16[4,2304,128]{2,1,0:T(8,128)(2,1)}, u32[]{:S(2)}) copy-start(bf16[4,2304,128]{2,1,0:T(8,128)(2,1)} %param.14) | copy-start | bytes 7077892
Sparse Core Ops, SparseCore 0:
  227.1 72.8 all-reduce.1
  473.7 101.9 reduce-scatter.3
